TPU v7x, 32 devices: a whole 2x2x4 slice. The times are simulated.
32 devices in a mesh: section: 4 (over x, core), dp: 8 (over z, y).
Axes of the slice: x: 2, y: 2, z: 4, core: 2. Of those that a mesh axis runs over, the one named last changes fastest.
Arguments:
- images: bfloat16 [16, 256, 768], P('dp'), may hold values from -6 to 6
- cotangent: bfloat16 [16, 256, 768], P('dp'), may hold values from -6 to 6
- kept_count: int32 [16], P('dp'), may hold values from 1 to 256, as said below
- kept_index: int32 [16, 256], P('dp'), may hold values from 0 to 255, as said below
- gain_one: bfloat16 [4, 768], P('section', 'dp'), may hold values from 0.5 to 1.5
- shift_one: bfloat16 [4, 768], P('section', 'dp'), may hold values from -1.5 to 1.5
- qkv_matrix: bfloat16 [4, 768, 2304], P('section', 'dp'), may hold values from -0.21875 to 0.21875
- qkv_shift: bfloat16 [4, 2304], P('section', 'dp'), may hold values from -1.5 to 1.5
- proj_matrix: bfloat16 [4, 768, 768], P('section', 'dp'), may hold values from -0.625 to 0.625
- proj_shift: bfloat16 [4, 768], P('section', 'dp'), may hold values from -1.5 to 1.5
- gain_two: bfloat16 [4, 768], P('section', 'dp'), may hold values from 0.5 to 1.5
- shift_two: bfloat16 [4, 768], P('section', 'dp'), may hold values from -1.5 to 1.5
- up_matrix: bfloat16 [4, 768, 3072], P('section', 'dp'), may hold values from -0.21875 to 0.21875
- up_shift: bfloat16 [4, 3072], P('section', 'dp'), may hold values from -1.5 to 1.5
- down_matrix: bfloat16 [4, 3072, 768], P('section', 'dp'), may hold values from -0.109375 to 0.109375
- down_shift: bfloat16 [4, 768], P('section', 'dp'), may hold values from -1.5 to 1.5
- frequency: bfloat16 [4, 768], P('section', 'dp'), may hold values from 0.049804688 to 1
Outputs:
- section_outputs: float32 [4, 16, 256, 768], P('section', 'dp')
- section_input_grads: float32 [4, 16, 256, 768], P('section', 'dp')
- gain_one_grad: float32 [4, 768], P('section', 'dp')
- shift_one_grad: float32 [4, 768], P('section', 'dp')
- qkv_matrix_grad: float32 [4, 768, 2304], P('section', 'dp')
- qkv_shift_grad: float32 [4, 2304], P('section', 'dp')
- proj_matrix_grad: float32 [4, 768, 768], P('section', 'dp')
- proj_shift_grad: float32 [4, 768], P('section', 'dp')
- gain_two_grad: float32 [4, 768], P('section', 'dp')
- shift_two_grad: float32 [4, 768], P('section', 'dp')
- up_matrix_grad: float32 [4, 768, 3072], P('section', 'dp')
- up_shift_grad: float32 [4, 3072], P('section', 'dp')
- down_matrix_grad: float32 [4, 3072, 768], P('section', 'dp')
- down_shift_grad: float32 [4, 768], P('section', 'dp')
- frequency_grad: float32 [4, 768], P('section', 'dp')
Inputs may be any that keep to these rules, and one draw needn't show every extreme that they name: `kept_count`: every image keeps at least one patch, and some image keeps all 256. `kept_index`: each row is a permutation of the 256 grid indices: slots below the image's kept_count hold its kept patches in rising order, the later slots the dropped ones in rising order.
All inputs are finite; a program needn't handle non-finite values.
Results may differ from a plain program's by a relative error of at most 0.025.
Values may be sent and summed in bfloat16 or wider, within the bound.
A program may use at most 256 MiB of HBM per device.

v0:
```python
import functools
import math

import jax
import jax.numpy as jnp
from jax import lax
from jax.experimental import pallas as pl
from jax.experimental.pallas import tpu as pltpu
from jax.sharding import PartitionSpec as P

D = 768
H = 12
HD = 64
GRID = 16
GRID_BITS = 4
EPSILON = 1e-06
MASKED = -1e30
GROUPS = 8
LANES = 128
TILE = 768
CHUNK = 64
GRAD_TILE = 768
GATHER_PARTS = (1, 3, 1, 6, 6)
AHEAD = 3
REDUCE_PARTS = ((4, 3), (3, 3), (1, 3), (2, 1), (0, 1))
WINDOW = 3
FINISH_STEPS = 2
LAG = 3
MESH = pl.DeviceIdType.MESH
F32 = jnp.float32
LOW = jnp.bfloat16


class Place:
    def __init__(self, replicas):
        section = lax.axis_index("section")
        dp = lax.axis_index("dp")
        self.replicas = replicas
        self.x, self.core = lax.div(section, 2), lax.rem(section, 2)
        group, self.m = lax.div(dp, replicas), lax.rem(dp, replicas)
        self.z, self.y = lax.div(group, 2), lax.rem(group, 2)
        self.half, self.odd = lax.div(self.z, 2), lax.rem(self.z, 2)
        self.role = 2 * self.x + self.odd
        self.mine = 2 * self.z + self.y
        self.home = self.core == self.odd
        self.away = self.core != self.odd

    def device(self, x, core, z, y):
        return (2 * x + core, (2 * z + y) * self.replicas + self.m)

    def sibling(self):
        return self.device(self.x, 1 - self.core, self.z, self.y)

    def across(self):
        return self.device(self.x, self.core, self.z, 1 - self.y)

    def along(self, k):
        return self.device(self.x, self.odd, self.core + 2 * k, self.y)

    def twin(self):
        return self.along(self.half)

    def is_self(self, k):
        return jnp.logical_and(self.home, self.half == k)

    def section(self, role):
        return self.device(
            lax.div(role, 2), self.core, 2 * self.half + lax.rem(role, 2), self.y
        )


def remote(source, target, send, arrive, to):
    return pltpu.make_async_remote_copy(
        src_ref=source,
        dst_ref=target,
        send_sem=send,
        recv_sem=arrive,
        device_id=to,
        device_id_type=MESH,
    )


def enter(at, sections):
    barrier = pltpu.get_barrier_semaphore()

    def greet(to):
        pl.semaphore_signal(barrier, inc=1, device_id=to, device_id_type=MESH)

    greet(at.sibling())
    greet(at.across())
    for k in range(2):

        @pl.when(jnp.logical_not(at.is_self(k)))
        def _():
            greet(at.along(k))

    @pl.when(at.role > 0)
    def _():
        greet(at.section(at.role - 1))

    @pl.when(at.role < sections - 1)
    def _():
        greet(at.section(at.role + 1))

    ends = jnp.where(jnp.logical_or(at.role == 0, at.role == sections - 1), 1, 0)
    pl.semaphore_wait(barrier, 6 - jnp.where(at.home, 1, 0) - ends)


def span(start, size):
    return pl.ds(pl.multiple_of(start, size), size)


def dot(a, b):
    return jnp.dot(a, b, preferred_element_type=F32)


def dot_nt(a, b):
    return lax.dot_general(a, b, (((1,), (1,)), ((), ())), preferred_element_type=F32)


def dot_tn(a, b):
    return lax.dot_general(a, b, (((0,), (0,)), ((), ())), preferred_element_type=F32)


def gather_pieces(sizes):
    pieces = []
    for n, (size, parts) in enumerate(zip(sizes, GATHER_PARTS)):
        rows = size // parts
        pieces += [(n, start, rows) for start in range(0, size, rows)]
    return pieces


def reduce_pieces(sizes):
    pieces = []
    for n, parts in REDUCE_PARTS:
        rows = sizes[n] // parts
        pieces += [(n, start, rows) for start in range(0, sizes[n], rows)]
    return pieces


def loop(count, body, unroll=1):
    def step(i, carry):
        body(i)
        return carry

    lax.fori_loop(0, count, step, 0, unroll=unroll)


SMALL_ROWS = 16


def quotient(values, divisor):
    return jnp.floor((values + 0.5) * (1.0 / divisor))


def selectors(size, first_row, index):
    group = quotient(index, size)
    inside = index - group * size
    row_in = quotient(inside, LANES)
    lane = inside - row_in * LANES
    row = group * SMALL_ROWS + as_float(first_row) + row_in
    ids = lax.broadcasted_iota(jnp.int32, (GROUPS * SMALL_ROWS, index.shape[1]), 0).astype(F32)
    return (ids == row).astype(F32), (ids == lane).astype(F32)


def positions(count):
    return lax.broadcasted_iota(jnp.int32, (1, count), 1).astype(F32)


def as_float(value):
    return lax.convert_element_type(value, F32)


def spread_positions():
    at = positions(D)
    pair = quotient(at, 2 * HD)
    return at - quotient(at, HD) * HD + pair * HD


def paired_positions():
    at = positions(D)
    pair = quotient(at, 2 * HD)
    inside = at - pair * (2 * HD)
    half = quotient(inside, HD)
    rest = inside - half * HD
    head = quotient(rest, HD // 2)
    return pair * (2 * HD) + head * HD + half * (HD // 2) + rest - head * (HD // 2)


def expand(block, size, first_row, index):
    rows, lanes = selectors(size, first_row, index)
    values = dot(block, lanes.astype(LOW))
    return jnp.sum(values * rows, axis=0, keepdims=True)


def fold(vector, size, first_row, index):
    rows, lanes = selectors(size, first_row, index)
    return lax.dot_general(
        rows * vector,
        lanes,
        (((1,), (1,)), ((), ())),
        precision=lax.Precision.HIGHEST,
        preferred_element_type=F32,
    )


def normalise(values):
    mean = jnp.mean(values, axis=-1, keepdims=True)
    centred = values - mean
    variance = jnp.mean(centred * centred, axis=-1, keepdims=True)
    scale = lax.rsqrt(variance + EPSILON)
    return centred * scale, scale


def pairing():
    shape = (2 * HD, 2 * HD)
    source = lax.broadcasted_iota(jnp.int32, shape, 0)
    target = lax.broadcasted_iota(jnp.int32, shape, 1)
    half, head = lax.div(target, HD), lax.rem(lax.div(target, HD // 2), 2)
    return jnp.where(
        source == head * HD + half * (HD // 2) + lax.rem(target, HD // 2), 1.0, 0.0
    ).astype(LOW)


def lanes_of(shape):
    return lax.broadcasted_iota(jnp.int32, shape, 1)


def first_half(shape):
    return jnp.bitwise_and(lanes_of(shape), 2 * HD - 1) < HD


def partner(values):
    pieces = [
        pltpu.roll(values[:, start : start + 2 * HD], HD, 1)
        for start in range(0, values.shape[1], 2 * HD)
    ]
    return jnp.concatenate(pieces, axis=1) if len(pieces) > 1 else pieces[0]


def unfold_turn(table):
    first, other = first_half(table.shape), partner(table)
    return jnp.where(first, table, other), jnp.where(first, -other, table)


LOG2_E = 1.0 / math.log(2.0)


def gelu_pair(u):
    phi = 0.5 * (1.0 + lax.erf(u * math.sqrt(0.5)))
    density = jnp.exp2(u * u * (-0.5 * LOG2_E)) * (1.0 / math.sqrt(2.0 * math.pi))
    return u * phi, phi + u * density


MATRICES = (2, 4, 8, 10)
VECTORS = (0, 1, 5, 6, 7, 11, 12, 3, 9)

GAIN_ONE, SHIFT_ONE, PROJ_SHIFT, GAIN_TWO, SHIFT_TWO, DOWN_SHIFT, FREQ_ROW, FREQ_COL = range(8)


def block_kernel(replicas, sections, images_here, patches, *refs):
    ins, refs = refs[:8], refs[8:]
    given, refs = refs[: len(VECTORS)], refs[len(VECTORS) :]
    outs, refs = refs[:7], refs[7:]
    qkv_part, proj_part, up_part, down_part, images, cotangent, counts, indices = ins
    result_out, grad_out_ref = outs[:2]
    totals = outs[2:]
    (
        small_w, qkv_w, proj_w, up_w, down_w,
        first_0, first_1, first_2, first_3, first_4,
        second_0, second_1, second_2, second_3, second_4,
        xin, gin, gcopy, fcol, frow, qkv, probs, att, mid, n2, act, slope, g1, wide,
        shipped, back_shipped, gat, turns, vec, qkv_b, up_b, vec_g, qkv_bg, up_bg, small_f,
        qkv_own, small_own, facts_own,
        gather_send, gather_arrive, near_send, near_arrive,
        across_send, across_arrive, along_send, along_arrive,
        swap_send, swap_arrive, pipe_send, pipe_arrive, ship_send, ship_arrive, load, token,
    ) = refs
    wholes = (small_w, qkv_w, proj_w, up_w, down_w)
    shares = (small_own, qkv_own, proj_part, up_part, down_part)
    firsts = (first_0, first_1, first_2, first_3, first_4)
    seconds = (second_0, second_1, second_2, second_3, second_4)
    partials = (small_f, qkv_w, proj_w, up_w, down_w)
    at = Place(replicas)
    last = sections - 1
    q = D // GROUPS

    own_qkv = pltpu.make_async_copy(qkv_part, qkv_own, load)
    own_qkv.start()
    small_f[...] = jnp.zeros_like(small_f)
    row = 0
    for vector_ref in given:
        size = vector_ref.shape[1]
        for start in range(0, size, LANES):
            width = min(LANES, size - start)
            small_f[row : row + 1, 0:width] = vector_ref[:, start : start + width].astype(F32)
            row += 1
    small_own[...] = small_f[0:SMALL_ROWS, :].astype(LOW)
    facts_own[...] = jnp.zeros_like(facts_own)
    for b in range(images_here):
        slot = lax.broadcasted_iota(jnp.int32, (1, patches), 1)
        index = indices[b : b + 1, :]
        facts_own[8 * b : 8 * b + 1, :] = jnp.where(slot < counts[b], 1.0, 0.0)
        facts_own[8 * b + 1 : 8 * b + 2, :] = as_float(lax.shift_right_logical(index, GRID_BITS))
        facts_own[8 * b + 2 : 8 * b + 3, :] = as_float(jnp.bitwise_and(index, GRID - 1))
    own_qkv.wait()
    for block_no in range(2 * H // 2):
        cols = slice(block_no * 2 * HD, (block_no + 1) * 2 * HD)
        qkv_own[:, cols] = dot(qkv_own[:, cols], pairing()).astype(LOW)

    enter(at, sections)

    def swap_copy(n, source, target):
        return remote(source, target, swap_send.at[n], swap_arrive.at[n], at.twin())

    def swap_local(n, source, target):
        return pltpu.make_async_copy(source, target, swap_arrive.at[n])

    every = at.core >= 0
    moves = (
        (0, facts_own, frow, every, every),
        (
            1, images, xin,
            jnp.logical_and(at.x == 0, at.core == 0),
            at.role == 0,
        ),
        (
            2, cotangent, gin,
            jnp.logical_and(at.x == last // 2, at.core == last % 2),
            at.role == last,
        ),
    )

    def swap_start(n):
        number, source, target, sends, takes = moves[n]

        @pl.when(jnp.logical_and(sends, at.home))
        def _():
            swap_local(number, source, target).start()

        @pl.when(jnp.logical_and(sends, at.away))
        def _():
            swap_copy(number, source, target).start()

    def swap_wait(n):
        number, source, target, sends, takes = moves[n]

        @pl.when(jnp.logical_and(takes, at.home))
        def _():
            swap_local(number, source, target).wait()

        @pl.when(jnp.logical_and(takes, at.away))
        def _():
            swap_copy(number, source, target).wait_recv()

    def swap_sent(n):
        number, source, target, sends, takes = moves[n]

        @pl.when(jnp.logical_and(sends, at.away))
        def _():
            swap_copy(number, source, target).wait_send()

    pieces = gather_pieces([share.shape[0] for share in shares])

    def block_of(ref, group):
        size = ref.shape[0] // GROUPS
        return ref.at[span(group * size, size), :]

    def piece_of(i, group):
        n, start, size = pieces[i]
        first = group * (wholes[n].shape[0] // GROUPS) + start
        return wholes[n].at[pl.ds(pl.multiple_of(first, 16), size), :]

    def share_of(i):
        n, start, size = pieces[i]
        return shares[n].at[pl.ds(start, size), :]

    def along(i, k):
        return remote(
            share_of(i), piece_of(i, at.mine),
            gather_send.at[i, k], gather_arrive.at[i, at.mine], at.along(k),
        )

    def own(i):
        return pltpu.make_async_copy(
            share_of(i), piece_of(i, at.mine), gather_arrive.at[i, at.mine]
        )

    def relay(i, slot, group, to):
        block = piece_of(i, group)
        return remote(block, block, gather_send.at[i, slot], gather_arrive.at[i, group], to)

    def gather_start(i):
        for k in range(2):

            @pl.when(at.is_self(k))
            def _():
                own(i).start()

            @pl.when(jnp.logical_not(at.is_self(k)))
            def _():
                along(i, k).start()

    def gather_started(i):
        for k in range(2):

            @pl.when(jnp.logical_not(at.is_self(k)))
            def _():
                along(i, k).wait_send()

    def gather_relay(i):
        for k in range(2):
            group = 2 * (at.core + 2 * k) + at.y

            @pl.when(at.is_self(k))
            def _():
                own(i).wait()

            @pl.when(jnp.logical_not(at.is_self(k)))
            def _():
                relay(i, 2 + k, group, at.sibling()).wait_recv()

            relay(i, 4 + k, group, at.across()).start()
            relay(i, 2 + k, group, at.sibling()).start()

    def gather_pass(i):
        for k in range(2):
            group = 2 * (at.core + 2 * k) + 1 - at.y
            relay(i, 6 + k, group, at.sibling()).wait_recv()
            relay(i, 6 + k, group, at.sibling()).start()

    def gather_wait(i):
        for k in range(2):
            for row in range(2):
                group = 2 * (1 - at.core + 2 * k) + row
                relay(i, 2 + k, group, at.sibling()).wait_recv()

    def gather_sent(i):
        for k in range(2):
            group = 2 * (at.core + 2 * k) + at.y
            other = 2 * (at.core + 2 * k) + 1 - at.y
            relay(i, 2 + k, group, at.sibling()).wait_send()
            relay(i, 4 + k, group, at.across()).wait_send()
            relay(i, 6 + k, other, at.sibling()).wait_send()

    count = len(pieces)

    def gather_step(i):
        gather_relay(i)
        gather_started(i)
        if i + AHEAD < count:
            gather_start(i + AHEAD)

    swap_start(0)
    gather_start(0)
    swap_start(1)
    for i in range(1, AHEAD):
        gather_start(i)
    gather_step(0)
    swap_wait(0)
    gather_pass(0)
    gather_wait(0)
    for b in range(images_here):
        filled = jnp.concatenate(
            [frow[8 * b : 8 * b + 8, :], jnp.zeros((LANES - 8, patches), F32)], axis=0
        )
        fcol[b * patches : (b + 1) * patches, :] = jnp.transpose(filled)

    block = small_w[...]
    plain = positions(D)
    apart = spread_positions()
    paired = paired_positions()

    def qkv_positions(t):
        return jnp.where(t < 2, paired, plain) + as_float(t) * D

    def take_vector(row):
        vec[row] = expand(block, q, row, plain)

    def take_frequency(t):
        vec[FREQ_ROW + t] = expand(block, q, FREQ_ROW, apart + as_float(t) * (D // 2))

    def take_qkv(t):
        qkv_b[:, span(t * D, D)] = expand(block, 3 * q, 7, qkv_positions(t))

    def take_up(t):
        up_b[:, span(t * D, D)] = expand(block, 4 * q, 10, plain + as_float(t) * D)

    loop(FREQ_ROW, take_vector)
    loop(2, take_frequency)
    loop(3, take_qkv)
    loop(4, take_up)
    vec_g[...] = jnp.zeros_like(vec_g)
    qkv_bg[...] = jnp.zeros_like(qkv_bg)
    up_bg[...] = jnp.zeros_like(up_bg)

    def vector(row):
        return vec[row]

    def vector_at(row, cols):
        return vec[row, :, cols]

    def tables(b):
        rows = span(b * patches, patches)
        facts = fcol[rows, :]
        row_at, col_at = facts[:, 1:2], facts[:, 2:3]
        first = first_half((patches, TILE))

        def piece(t):
            cols = span(t * TILE, TILE)
            angle = row_at * vector_at(FREQ_ROW, cols) + col_at * vector_at(FREQ_COL, cols)
            turns[rows, cols] = jnp.where(first, jnp.cos(angle), jnp.sin(angle))

        loop(D // TILE, piece)

    def ship_start(n, b, source, target):
        rows = span(b * patches, patches)

        @pl.when(at.home)
        def _():
            ship_here(n, b, source, target).start()

        @pl.when(at.away)
        def _():
            ship_away(n, b, source, target).start()

    def ship_here(n, b, source, target):
        rows = span(b * patches, patches)
        return pltpu.make_async_copy(
            source.at[rows, :], target.at[rows, :], ship_arrive.at[n, b]
        )

    def ship_away(n, b, source, target):
        rows = span(b * patches, patches)
        return remote(
            source.at[rows, :], target.at[rows, :],
            ship_send.at[n, b], ship_arrive.at[n, b], at.twin(),
        )

    def ship_wait(n, b, source, target):
        @pl.when(at.home)
        def _():
            ship_here(n, b, source, target).wait()

        @pl.when(at.away)
        def _():
            ship_away(n, b, source, target).wait_recv()
            ship_away(n, b, source, target).wait_send()

    def pipe(n, b, target, role):
        rows = span(b * patches, patches)
        source = shipped if n == 0 else back_shipped
        return remote(
            source.at[rows, :], target.at[rows, :],
            pipe_send.at[n, b], pipe_arrive.at[n, b], at.section(role),
        )

    def chunks(b, body):
        loop(
            patches // CHUNK,
            lambda i: body(span(b * patches + i * CHUNK, CHUNK), span(i * CHUNK, CHUNK)),
            unroll=patches // CHUNK,
        )

    def own_lanes(e):
        inside = jnp.bitwise_and(lanes_of((patches, 2 * HD)), HD - 1) < HD // 2
        return inside if e == 0 else jnp.logical_not(inside)

    def value_lanes(e):
        inside = lanes_of((patches, 2 * HD)) < HD
        return inside if e == 0 else jnp.logical_not(inside)

    def rows_at(b):
        return span(b * patches, patches)

    def attention_inputs(b):
        rows = rows_at(b)

        def norm_one(here, inside):
            hat, _ = normalise(xin[here, :].astype(F32))
            shipped[here, :] = (hat * vector(GAIN_ONE) + vector(SHIFT_ONE)).astype(LOW)

        chunks(b, norm_one)

        def turn(t):
            cols = span(t * D, D)
            raw = dot(shipped[rows, :], qkv_w[:, cols]) + qkv_b[:, cols]
            cosine, sine = unfold_turn(turns[rows, :])
            turned = raw * cosine + partner(raw) * sine
            qkv[rows, cols] = turned.astype(LOW)

        loop(2, turn, unroll=2)
        cols = pl.ds(2 * D, D)
        qkv[rows, cols] = (dot(shipped[rows, :], qkv_w[:, cols]) + qkv_b[:, cols]).astype(LOW)

    def attention(b, unroll=H // 2):
        rows = rows_at(b)
        barred = jnp.where(frow[span(b * 8, 8), :][0:1, :] > 0, 0.0, MASKED)

        def heads(pair):
            cols = span(pair * 2 * HD, 2 * HD)
            query = qkv[rows, cols]
            key = qkv[rows, span(D + pair * 2 * HD, 2 * HD)]
            value = qkv[rows, span(2 * D + pair * 2 * HD, 2 * HD)]
            value = jnp.concatenate([value, jnp.ones_like(value)], axis=1)
            found = []
            for e in range(2):
                own_query = jnp.where(own_lanes(e), query, jnp.zeros_like(query))
                scores = dot_nt(own_query, key) * (HD ** (-0.5) * LOG2_E) + barred
                powers = jnp.exp2(scores - jnp.max(scores, axis=1, keepdims=True))
                both = dot(powers.astype(LOW), value)
                share = 1.0 / both[:, 2 * HD :]
                probs[b * H + 2 * pair + e] = (
                    powers * jnp.concatenate([share] * (patches // (2 * HD)), axis=1)
                ).astype(LOW)
                found.append(both[:, : 2 * HD] * share)
            att[rows, cols] = jnp.where(value_lanes(0), found[0], found[1]).astype(LOW)

        loop(H // 2, heads, unroll=unroll)

    def middle(b):
        rows = rows_at(b)
        keep_col = fcol[rows, :][:, 0:1]
        branch = dot(att[rows, :], proj_w[...]) + vector(PROJ_SHIFT)
        mid[rows, :] = xin[rows, :].astype(F32) + keep_col * branch

        def norm_two(here, inside):
            hat, _ = normalise(mid[here, :])
            n2[here, :] = (hat * vector(GAIN_TWO) + vector(SHIFT_TWO)).astype(LOW)

        chunks(b, norm_two)

    def raised(b, pieces_now=1):
        rows = rows_at(b)
        tile = up_w.shape[1] // pieces_now

        def part(t):
            cols = span(t * tile, tile)
            hidden = dot(n2[rows, :], up_w[:, cols]) + up_b[:, cols]
            value, gradient = gelu_pair(hidden)
            act[rows, cols] = value.astype(LOW)
            slope[rows, cols] = gradient.astype(LOW)

        if pieces_now == 1:
            part(0)
        else:
            loop(pieces_now, part)

    def lowered(b):
        rows = rows_at(b)
        keep_col = fcol[rows, :][:, 0:1]
        branch = dot(act[rows, :], down_w[...]) + vector(DOWN_SHIFT)
        shipped[rows, :] = (mid[rows, :] + keep_col * branch).astype(LOW)

    def piece_range(n):
        return [i for i, piece in enumerate(pieces) if piece[0] == n]

    def ready(n):
        for i in piece_range(n):
            gather_wait(i)

    def section_zero(stage_now):
        @pl.when(at.role == 0)
        def _():
            loop(images_here, stage_now)

    ready_qkv = LAG + piece_range(1)[-1]
    slots = {
        1: (None, tables),
        ready_qkv: (1, attention_inputs),
        ready_qkv + 2: (None, lambda b: attention(b, 3)),
        ready_qkv + 4: (2, middle),
        LAG + piece_range(3)[-1]: (3, lambda b: raised(b, 4)),
    }
    for i in range(1, count + LAG):
        if i < count:
            gather_step(i)
        if 1 <= i - LAG:
            gather_pass(i - LAG)
        if i == piece_range(1)[-1]:
            swap_wait(1)
        if i in slots:
            matrix, stage_now = slots[i]
            if matrix is not None:
                ready(matrix)
            if stage_now is tables:
                loop(images_here, tables)
            else:
                section_zero(stage_now)
    swap_start(2)
    ready(4)

    def pass_token():
        pl.semaphore_signal(token, inc=1, device_id=at.sibling(), device_id_type=MESH)

    def send_on(b):
        pipe(0, b, xin, at.role + 1).start()

    @pl.when(at.role == 0)
    def _():
        def lower_and_send(b):
            lowered(b)

            @pl.when(jnp.logical_and(at.core == 0, b == 0))
            def _():
                send_on(b)

        loop(images_here, lower_and_send)
        for b in range(images_here):

            @pl.when(at.core == 0)
            def _():
                if b > 0:
                    pl.semaphore_wait(token, 1)
                    send_on(b)
                pipe(0, b, xin, at.role + 1).wait_send()
                pass_token()

            @pl.when(at.core == 1)
            def _():
                pl.semaphore_wait(token, 1)
                send_on(b)
                pipe(0, b, xin, at.role + 1).wait_send()
                if b < images_here - 1:
                    pass_token()

    @pl.when(at.role > 0)
    def _():
        def forward(b):
            pipe(0, b, xin, at.role - 1).wait_recv()
            for stage_now in (attention_inputs, attention, middle, raised, lowered):
                stage_now(b)

            @pl.when(at.role < last)
            def _():
                send_on(b)

        loop(images_here, forward)
        for b in range(images_here):

            @pl.when(at.role < last)
            def _():
                pipe(0, b, xin, at.role + 1).wait_send()

    for b in range(images_here):
        ship_start(0, b, shipped, result_out)
    swap_wait(2)
    for n in range(3):
        swap_sent(n)
    for i in range(count):
        gather_sent(i)

    def norm_back(values, gain_row, grad):
        hat, scale = normalise(values)
        vec_g[gain_row] += jnp.sum(grad * hat, axis=0, keepdims=True)
        vec_g[gain_row + 1] += jnp.sum(grad, axis=0, keepdims=True)
        inner = grad * vector(gain_row)
        along_hat = jnp.mean(inner * hat, axis=-1, keepdims=True)
        level = jnp.mean(inner, axis=-1, keepdims=True)
        return scale * (inner - level - hat * along_hat), hat

    def add_row(ref, cols, values):
        ref[:, cols] += jnp.sum(values.astype(F32), axis=0, keepdims=True)

    def hidden_back(b):
        rows = rows_at(b)

        def mask_coming(here, inside):
            coming = gin[here, :].astype(F32)
            gcopy[inside, :] = gin[here, :]
            grad_two = (coming * fcol[here, :][:, 0:1]).astype(LOW)
            gin[here, :] = grad_two
            vec_g[DOWN_SHIFT] += jnp.sum(grad_two.astype(F32), axis=0, keepdims=True)

        chunks(b, mask_coming)
        grad = dot_nt(gin[rows, :], down_w[...])
        low = (grad * slope[rows, :].astype(F32)).astype(LOW)
        slope[rows, :] = low
        up_bg[...] += jnp.sum(low.astype(F32), axis=0, keepdims=True)
        wide[...] = dot_nt(slope[rows, :], up_w[...])

    def middle_back(b):
        rows = rows_at(b)

        def norm_two_back(here, inside):
            part, _ = norm_back(mid[here, :], GAIN_TWO, wide[inside, :])
            grad_mid = gcopy[inside, :].astype(F32) + part
            mid[here, :] = grad_mid
            grad_one = (grad_mid * fcol[here, :][:, 0:1]).astype(LOW)
            g1[here, :] = grad_one
            vec_g[PROJ_SHIFT] += jnp.sum(grad_one.astype(F32), axis=0, keepdims=True)

        chunks(b, norm_two_back)
        gat[...] = dot_nt(g1[rows, :], proj_w[...]).astype(LOW)

    def attention_back(b):
        rows = rows_at(b)
        facts = fcol[rows, :]
        row_at, col_at = facts[:, 1:2], facts[:, 2:3]
        lane_from = lax.broadcasted_iota(jnp.int32, (4 * HD, 4 * HD), 0)
        lane_to = lax.broadcasted_iota(jnp.int32, (4 * HD, 4 * HD), 1)
        same = lax.rem(lax.div(lane_from, HD), 2) == lax.div(lane_to, 2 * HD)
        head_sums = jnp.where(same, 1.0, 0.0).astype(LOW)

        def heads(pair):
            cols = span(pair * 2 * HD, 2 * HD)
            key_cols = span(D + pair * 2 * HD, 2 * HD)
            value_cols = span(2 * D + pair * 2 * HD, 2 * HD)
            query, key, value = qkv[rows, cols], qkv[rows, key_cols], qkv[rows, value_cols]
            grad = gat[:, cols]
            product = grad.astype(F32) * att[rows, cols].astype(F32)
            high = product.astype(LOW)
            rest = (product - high.astype(F32)).astype(LOW)
            centres = dot(jnp.concatenate([high, rest], axis=1), head_sums)
            to_q, to_k, to_v = [], [], []
            for e in range(2):
                own_grad = jnp.where(value_lanes(e), grad, jnp.zeros_like(grad))
                soft_low = probs[b * H + 2 * pair + e]
                soft = soft_low.astype(F32)
                grad_soft = dot_nt(own_grad, value)
                centre = centres[:, e * 2 * HD : (e + 1) * 2 * HD]
                centre = jnp.concatenate([centre] * (patches // (2 * HD)), axis=1)
                grad_scores = (soft * (grad_soft - centre)).astype(LOW)
                to_q.append(dot(grad_scores, key))
                to_k.append(dot_tn(grad_scores, query))
                to_v.append(dot_tn(soft_low, grad))
            scale = HD ** (-0.5)
            turned_q = jnp.where(own_lanes(0), to_q[0], to_q[1]) * scale
            turned_k = jnp.where(own_lanes(0), to_k[0], to_k[1]) * scale
            grad_v = jnp.where(value_lanes(0), to_v[0], to_v[1]).astype(LOW)
            cosine, sine = unfold_turn(turns[rows, cols])
            other_q, other_k = partner(turned_q), partner(turned_k)
            sign = jnp.where(first_half((1, 2 * HD)), 1.0, -1.0)
            swing = sign * (other_q * query.astype(F32) + other_k * key.astype(F32))
            for n, place_at in enumerate((row_at, col_at)):
                vec_g[FREQ_ROW + n, :, cols] += jnp.sum(swing * place_at, axis=0, keepdims=True)
            grad_q = (turned_q * cosine - other_q * sine).astype(LOW)
            grad_k = (turned_k * cosine - other_k * sine).astype(LOW)
            for where, low in ((cols, grad_q), (key_cols, grad_k), (value_cols, grad_v)):
                qkv[rows, where] = low
                add_row(qkv_bg, where, low)

        loop(H // 2, heads, unroll=H // 2)

    def source_back(b):
        rows = rows_at(b)
        wide[...] = dot_nt(qkv[rows, :], qkv_w[...])

        def norm_one_back(here, inside):
            part, hat = norm_back(xin[here, :].astype(F32), GAIN_ONE, wide[inside, :])
            xin[here, :] = (hat * vector(GAIN_ONE) + vector(SHIFT_ONE)).astype(LOW)
            back_shipped[here, :] = (mid[here, :] + part).astype(LOW)

        chunks(b, norm_one_back)

        @pl.when(at.role > 0)
        def _():
            pipe(1, b, gin, at.role - 1).start()

        @pl.when(at.role == 0)
        def _():
            ship_start(1, b, back_shipped, grad_out_ref)

    def backward_wait(b):
        @pl.when(at.role < last)
        def _():
            pipe(1, b, gin, at.role + 1).wait_recv()

    parts = reduce_pieces([partial.shape[0] // GROUPS for partial in partials])

    def to_sibling(n, slot):
        k, other = slot % 2, slot < 2
        group = 2 * (1 - at.core + 2 * k) + (1 - at.y if other else at.y)
        return remote(
            block_of(partials[n], group), firsts[n].at[slot],
            near_send.at[n, slot], near_arrive.at[n, slot], at.sibling(),
        )

    def held(slot):
        k, other = slot % 2, slot < 2
        return 2 * (at.core + 2 * k) + (1 - at.y if other else at.y)

    def held_part(p, slot):
        n, start, size = parts[p]
        first = held(slot) * (partials[n].shape[0] // GROUPS) + start
        return partials[n].at[pl.ds(pl.multiple_of(first, 16), size), :]

    def to_across(p, k):
        n, start, size = parts[p]
        return remote(
            held_part(p, k), seconds[n].at[k, pl.ds(start, size), :],
            across_send.at[p, k], across_arrive.at[p, k], at.across(),
        )

    def landing(p, half):
        n, start, size = parts[p]
        return totals[n].at[half, pl.ds(start, size), :]

    def to_owner(p, k):
        return remote(
            held_part(p, 2 + k), landing(p, at.half),
            along_send.at[p, k], along_arrive.at[p, at.half], at.along(k),
        )

    def to_self(p, k):
        return pltpu.make_async_copy(
            held_part(p, 2 + k), landing(p, k), along_arrive.at[p, k]
        )

    def from_other(p, k):
        return remote(
            held_part(p, 2 + k), landing(p, k),
            along_send.at[p, k], along_arrive.at[p, k], at.along(k),
        )

    def add(p, slot, source, index):
        n, start, size = parts[p]
        ref = partials[n]
        base = held(slot) * (ref.shape[0] // GROUPS) + start
        step = 16

        def body(i):
            here = pl.ds(pl.multiple_of(base + i * step, step), step)
            there = pl.ds(pl.multiple_of(start + i * step, step), step)
            total = ref[here, :].astype(F32) + source[index, there, :].astype(F32)
            ref[here, :] = total.astype(ref.dtype)

        loop(size // step, body)

    def reduce_start(n):
        for slot in range(4):
            to_sibling(n, slot).start()

    def reduce_across(p):
        n, start, size = parts[p]
        if start == 0:
            for slot in range(4):
                to_sibling(n, slot).wait_recv()
        for slot in range(2):
            add(p, slot, firsts[n], slot)
        for k in range(2):
            if p >= WINDOW:
                to_across(p - WINDOW, k).wait_send()
            to_across(p, k).start()
        for slot in range(2, 4):
            add(p, slot, firsts[n], slot)

    def reduce_along(p):
        n, start, size = parts[p]
        for k in range(2):
            to_across(p, k).wait_recv()
            add(p, 2 + k, seconds[n], k)

            @pl.when(jnp.logical_not(at.is_self(k)))
            def _():
                to_owner(p, k).start()

            @pl.when(at.is_self(k))
            def _():
                to_self(p, k).start()

    def down_grad(width):
        def tile(t):
            cols = span(t * width, width)
            down_w[cols, :] = dot_tn(act[:, cols], gin[...]).astype(LOW)

        loop(down_w.shape[0] // width, tile)
        reduce_start(4)

    def up_grad(width):
        def tile(t):
            cols = span(t * width, width)
            up_w[:, cols] = dot_tn(n2[...], slope[:, cols]).astype(LOW)

        loop(up_w.shape[1] // width, tile)
        reduce_start(3)

    def proj_grad():
        proj_w[...] = dot_tn(att[...], g1[...]).astype(LOW)
        reduce_start(2)

    def qkv_grad():
        for block_no in range(2 * H // 2):
            cols = slice(block_no * 2 * HD, (block_no + 1) * 2 * HD)
            qkv[:, cols] = dot_nt(qkv[:, cols], pairing()).astype(LOW)

        def tile(t):
            cols = span(t * D, D)
            qkv_w[:, cols] = dot_tn(xin[...], qkv[:, cols]).astype(LOW)

        loop(qkv_w.shape[1] // D, tile)
        reduce_start(1)

    def vector_grads():
        small_f[...] = jnp.zeros_like(small_f)

        def give_vector(row):
            small_f[...] += fold(vec_g[row], q, row, plain)

        def give_frequency(t):
            small_f[...] += fold(vec_g[FREQ_ROW + t], q, FREQ_ROW, apart + as_float(t) * (D // 2))

        def give_qkv(t):
            small_f[...] += fold(qkv_bg[:, span(t * D, D)], 3 * q, 7, qkv_positions(t))

        def give_up(t):
            small_f[...] += fold(up_bg[:, span(t * D, D)], 4 * q, 10, plain + as_float(t) * D)

        loop(FREQ_ROW, give_vector)
        loop(2, give_frequency)
        loop(3, give_qkv)
        loop(4, give_up)
        reduce_start(0)

    def early_grads(width):
        down_grad(width)
        reduce_across(0)
        up_grad(width)
        for p in range(1, WINDOW):
            reduce_across(p)

    def backward(b):
        backward_wait(b)
        hidden_back(b)

        @pl.when(jnp.logical_and(at.role == 0, b == images_here - 1))
        def _():
            early_grads(GRAD_TILE)

        middle_back(b)
        attention_back(b)
        source_back(b)

    loop(images_here, backward)

    @pl.when(at.role > 0)
    def _():
        early_grads(GRAD_TILE // 2)

    qkv_grad()
    reduce_across(WINDOW)
    proj_grad()
    vector_grads()
    for b in range(images_here):

        @pl.when(at.role > 0)
        def _():
            pipe(1, b, gin, at.role - 1).wait_send()
            ship_start(1, b, back_shipped, grad_out_ref)

    for p in range(len(parts)):
        if p + WINDOW + 1 < len(parts):
            reduce_across(p + WINDOW + 1)
        reduce_along(p)

    for b in range(images_here):
        ship_wait(0, b, shipped, result_out)
        ship_wait(1, b, back_shipped, grad_out_ref)
    for n in range(5):
        for slot in range(4):
            to_sibling(n, slot).wait_send()
    for p in range(len(parts)):
        for k in range(2):
            if p >= len(parts) - WINDOW:
                to_across(p, k).wait_send()

            @pl.when(jnp.logical_not(at.is_self(k)))
            def _():
                to_owner(p, k).wait_send()
                from_other(p, k).wait_recv()

            @pl.when(at.is_self(k))
            def _():
                to_self(p, k).wait()


def run_block(replicas, sections, matrices, images, cotangent, counts, indices, vectors):
    images_here, patches = images.shape[:2]
    rows = images_here * patches
    hidden = matrices[2].shape[1]
    anywhere = pl.BlockSpec(memory_space=pl.ANY)
    vmem, dma = pltpu.VMEM, pltpu.SemaphoreType.DMA
    inside = pl.BlockSpec(memory_space=vmem)
    flat = [value.reshape(rows, D) for value in (images, cotangent)]
    shapes = [(SMALL_ROWS, LANES)] + [matrix.shape for matrix in matrices]
    kinds = [F32] + [LOW] * 4
    outs = [jax.ShapeDtypeStruct((rows, D), LOW)] * 2
    outs += [jax.ShapeDtypeStruct((2, *shape), kind) for shape, kind in zip(shapes, kinds)]

    reduce_count = sum(parts for _, parts in REDUCE_PARTS)

    def buffers(slots):
        return [vmem((slots, *shape), kind) for shape, kind in zip(shapes, kinds)]

    scratch = [vmem((GROUPS * shape[0], shape[1]), LOW) for shape in shapes]
    scratch += buffers(4) + buffers(2)
    scratch += [
        vmem((rows, D), LOW),
        vmem((rows, D), LOW),
        vmem((patches, D), LOW),
        vmem((rows, LANES), F32),
        vmem((images_here * 8, patches), F32),
        vmem((rows, 3 * D), LOW),
        vmem((images_here * H, patches, patches), LOW),
        vmem((rows, D), LOW),
        vmem((rows, D), F32),
        vmem((rows, D), LOW),
        vmem((rows, hidden), LOW),
        vmem((rows, hidden), LOW),
        vmem((rows, D), LOW),
        vmem((patches, D), F32),
        vmem((rows, D), LOW),
        vmem((rows, D), LOW),
        vmem((patches, D), LOW),
        vmem((rows, D), F32),
        vmem((8, 1, D), F32),
        vmem((1, 3 * D), F32),
        vmem((1, hidden), F32),
        vmem((8, 1, D), F32),
        vmem((1, 3 * D), F32),
        vmem((1, hidden), F32),
        vmem((GROUPS * SMALL_ROWS, LANES), F32),
        vmem(matrices[0].shape, LOW),
        vmem((SMALL_ROWS, LANES), LOW),
        vmem((images_here * 8, patches), F32),
        dma((sum(GATHER_PARTS), 8)),
        dma((sum(GATHER_PARTS), GROUPS)),
        dma((5, 4)),
        dma((5, 4)),
        dma((reduce_count, 2)),
        dma((reduce_count, 2)),
        dma((reduce_count, 2)),
        dma((reduce_count, 2)),
        dma((3,)),
        dma((3,)),
        dma((2, images_here)),
        dma((2, images_here)),
        dma((2, images_here)),
        dma((2, images_here)),
        dma,
        pltpu.SemaphoreType.REGULAR,
    ]
    results = pl.pallas_call(
        functools.partial(block_kernel, replicas, sections, images_here, patches),
        out_shape=outs,
        in_specs=[anywhere] * 6
        + [pl.BlockSpec(memory_space=pltpu.SMEM), inside]
        + [inside] * len(vectors),
        out_specs=[anywhere] * 7,
        scratch_shapes=scratch,
        compiler_params=pltpu.CompilerParams(
            collective_id=0, has_side_effects=True, vmem_limit_bytes=63 * 1024 * 1024
        ),
        name="block",
    )(*matrices, *flat, counts, indices, *vectors)
    finished = finish(results, [vector.shape[1] for vector in vectors])
    outputs, input_grads = (value.reshape(images.shape) for value in finished[:2])
    return outputs, input_grads, finished[2:6], finished[6:]


def finish_kernel(sizes, *refs):
    result, grad, small, *pairs = refs[:7]
    result_out, grad_out, *outs = refs[7:]
    result_out[...] = result[...].astype(F32)
    grad_out[...] = grad[...].astype(F32)
    for pair, out in zip(pairs, outs[:4]):
        out[...] = pair[0].astype(F32) + pair[1].astype(F32)

    @pl.when(pl.program_id(0) == 0)
    def _():
        row = 0
        for size, out in zip(sizes, outs[4:]):
            for start in range(0, size, LANES):
                width = min(LANES, size - start)
                out[:, start : start + width] = (
                    small[0, row : row + 1, 0:width] + small[1, row : row + 1, 0:width]
                )
                row += 1


def finish(values, sizes):
    steps = FINISH_STEPS
    rows = values[0].shape[0]
    whole = pl.BlockSpec((rows // steps, D), lambda i: (i, 0))
    ins, outs, shapes = [whole] * 2, [whole] * 2, [(rows, D)] * 2
    ins.append(pl.BlockSpec(values[2].shape, lambda i: (0, 0, 0)))
    for pair in values[3:]:
        _, size, width = pair.shape
        ins.append(pl.BlockSpec((2, size // steps, width), lambda i: (0, i, 0)))
        outs.append(pl.BlockSpec((size // steps, width), lambda i: (i, 0)))
        shapes.append((size, width))
    for size in sizes:
        outs.append(pl.BlockSpec((1, size), lambda i: (0, 0)))
        shapes.append((1, size))
    return pl.pallas_call(
        functools.partial(finish_kernel, sizes),
        grid=(steps,),
        out_shape=[jax.ShapeDtypeStruct(shape, F32) for shape in shapes],
        in_specs=ins,
        out_specs=outs,
        compiler_params=pltpu.CompilerParams(vmem_limit_bytes=63 * 1024 * 1024),
        name="finish",
    )(*values)


def local(images, cotangent, kept_count, kept_index, *weights):
    sections = lax.axis_size("section")
    replicas = lax.axis_size("dp") // GROUPS
    subgroups = [[g * replicas + r for r in range(replicas)] for g in range(GROUPS)]
    if replicas > 1:
        weights = tuple(
            lax.all_gather(value, "dp", axis=1, tiled=True, axis_index_groups=subgroups)
            for value in weights
        )
    matrices = [weights[n][0] for n in MATRICES]
    vectors = [weights[n] for n in VECTORS]
    outputs, input_grads, sums, vector_sums = run_block(
        replicas, sections, matrices, images, cotangent, kept_count, kept_index, vectors
    )
    grads = [None] * len(weights)
    for n, value in zip(MATRICES, sums):
        grads[n] = value
    for n, vector in zip(VECTORS, vector_sums):
        grads[n] = vector[0]
    if replicas > 1:
        grads = [
            lax.psum_scatter(
                value, "dp", scatter_dimension=0, tiled=True, axis_index_groups=subgroups
            )
            for value in grads
        ]
    return (outputs[None], input_grads[None], *(value[None] for value in grads))


def solution(mesh):
    in_specs = (
        P("dp", None, None),
        P("dp", None, None),
        P("dp"),
        P("dp", None),
        P("section", "dp"),
        P("section", "dp"),
        P("section", "dp", None),
        P("section", "dp"),
        P("section", "dp", None),
        P("section", "dp"),
        P("section", "dp"),
        P("section", "dp"),
        P("section", "dp", None),
        P("section", "dp"),
        P("section", "dp", None),
        P("section", "dp"),
        P("section", "dp"),
    )
    out_specs = (
        P("section", "dp", None, None),
        P("section", "dp", None, None),
        P("section", "dp"),
        P("section", "dp"),
        P("section", "dp", None),
        P("section", "dp"),
        P("section", "dp", None),
        P("section", "dp"),
        P("section", "dp"),
        P("section", "dp"),
        P("section", "dp", None),
        P("section", "dp"),
        P("section", "dp", None),
        P("section", "dp"),
        P("section", "dp"),
    )
    return jax.shard_map(local, mesh=mesh, in_specs=in_specs, out_specs=out_specs, check_vma=False)
```

profile of v0, /device:TPU:17, one launch (start us, length us, event | category | flops | bytes accessed | tf_op | source)
XLA Modules:
  0.0 329.3 jit_solution(9817487039623092313)
XLA Ops:
  0.7 323.7 %block.1 = (bf16[512,768]{1,0:T(8,128)(2,1)}, bf16[512,768]{1,0:T(8,128)(2,1)}, f32[2,16,128]{2,1,0:T(8,128)}, bf16[2,96,2304]{2,1,0:T(8,128)(2,1)}, bf16[2,96,7...) custom-call(bf16[96,2304]{1,0:T(8,128)(2,1)} %bitcast.16, bf16[96,768]{1,0:T(8,128)(2,1)} %bitcast.17, ...), custom_call_target="tpu_custom_call" | custom-call | tf_op jit(solution)/shard_map/block/pallas_call | solution.py:1143
  324.3 4.8 %finish.1 = (f32[512,768]{1,0:T(8,128)}, f32[512,768]{1,0:T(8,128)}, f32[96,2304]{1,0:T(8,128)}, f32[96,768]{1,0:T(8,128)}, f32[96,3072]{1,0:T(8,128)}, /*index=...) custom-call(bf16[512,768]{1,0:T(8,128)(2,1)} %get-tuple-element.37.r, ...), custom_call_target="tpu_custom_call" | custom-call | tf_op jit(solution)/shard_map/finish/pallas_call | solution.py:1195
where the time goes:
time: 335 us; the launch traced here: 329 us
  Pallas kernels  328 us (98%)
    pallas_call x1, Pallas kernels, run_block(): pl.pallas_call(functools.partial(block_kernel, replicas, sections, images...  324 us

commit v1 on v0

--- a/solution.py
+++ b/solution.py
@@ -668,7 +668,7 @@
     slots = {
         1: (None, tables),
         ready_qkv: (1, attention_inputs),
-        ready_qkv + 2: (None, lambda b: attention(b, 3)),
+        ready_qkv + 2: (None, lambda b: attention(b, 2)),
         ready_qkv + 4: (2, middle),
         LAG + piece_range(3)[-1]: (3, lambda b: raised(b, 4)),
     }
@@ -1035,7 +1035,7 @@
 
     @pl.when(at.role > 0)
     def _():
-        early_grads(GRAD_TILE // 2)
+        early_grads(GRAD_TILE)
 
     qkv_grad()
     reduce_across(WINDOW)

time: 335 us -> 333 us (level)
  no operation moved by 1% of the time
where the time goes in v1:
time: 333 us; the launch traced here: 329 us
  Pallas kernels  328 us (98%)
    pallas_call x1, Pallas kernels, run_block(): pl.pallas_call(functools.partial(block_kernel, replicas, sections, images...  323 us

profile of v1, /device:TPU:17, one launch (start us, length us, event | category | flops | bytes accessed | tf_op | source)
XLA Modules:
  0.0 328.6 jit_solution(12049798812020591906)
XLA Ops:
  0.7 323.0 %block.1 = (bf16[512,768]{1,0:T(8,128)(2,1)}, bf16[512,768]{1,0:T(8,128)(2,1)}, f32[2,16,128]{2,1,0:T(8,128)}, bf16[2,96,2304]{2,1,0:T(8,128)(2,1)}, bf16[2,96,7...) custom-call(bf16[96,2304]{1,0:T(8,128)(2,1)} %bitcast.16, bf16[96,768]{1,0:T(8,128)(2,1)} %bitcast.17, ...), custom_call_target="tpu_custom_call" | custom-call | tf_op jit(solution)/shard_map/block/pallas_call | solution.py:1143
  323.6 4.8 %finish.1 = (f32[512,768]{1,0:T(8,128)}, f32[512,768]{1,0:T(8,128)}, f32[96,2304]{1,0:T(8,128)}, f32[96,768]{1,0:T(8,128)}, f32[96,3072]{1,0:T(8,128)}, /*index=...) custom-call(bf16[512,768]{1,0:T(8,128)(2,1)} %get-tuple-element.37.r, ...), custom_call_target="tpu_custom_call" | custom-call | tf_op jit(solution)/shard_map/finish/pallas_call | solution.py:1195
